TPU v7x, 256 devices: a whole 4x4x8 slice. The times are simulated.
256 devices in a mesh: occ: 64 (over y, z, x_lo), virt: 4 (over x_hi, core).
Axes of the slice: x: 4 (x_hi: 2, x_lo: 2; x = x_hi * 2 + x_lo), y: 4, z: 8, core: 2. Of those that a mesh axis runs over, the one named last changes fastest.
Arguments:
- integrals: bfloat16 [64, 1024, 1536], P('occ', 'virt'), may hold values from -2 to 2
- occupied_energy: float32 [64], replicated, may hold values from -2 to -0.2
- virtual_energy: float32 [1024], replicated, may hold values from 0.5 to 4
- partner_list: int32 [2, 64], replicated, may hold values from 0 to 63, each once within a row
- tile_lists: int32 [2, 64, 4, 56], P(None, 'occ', 'virt'), may hold values from -1 to 63, as said below
Outputs:
- gradient: float32 [64, 1024, 1536], P('occ', 'virt')
Inputs may be any that keep to these rules, and one draw needn't show every extreme that they name: Each row partner_list[k] holds every block number once. In each list tile_lists[k, d, s] the live entries stand first, are distinct, and number from 24 to 56; the rest are -1. For each k and d one slice s holds exactly 56 live entries.
All inputs are finite; a program needn't handle non-finite values.
Results may differ from a plain program's by a relative error of at most 0.0021.
Values may be sent and summed in bfloat16 or wider, within the bound.
A program may use at most 64 MiB of HBM per device.

v0:
```python
import math

import jax
import jax.numpy as jnp
from jax import lax
from jax.sharding import PartitionSpec as P

TILE = 64


def to_tiles(source, tile_width):
    orbitals, row_count, aux_width = source.shape
    tile_count = row_count // tile_width
    shaped = source.reshape(orbitals, tile_count, tile_width, aux_width)
    return shaped.transpose(1, 0, 2, 3).reshape(tile_count, orbitals * tile_width, aux_width)


def split_pieces(source, piece_count):
    orbitals, row_count, aux_width = source.shape
    return source.reshape(orbitals, piece_count, row_count // piece_count, aux_width)


def join_pieces(pieces):
    orbitals, piece_count, row_count, aux_width = pieces.shape
    return pieces.reshape(orbitals, piece_count * row_count, aux_width)


def one_hot(indices, width, dtype):
    return (indices[:, None] == jnp.arange(width, dtype=jnp.int32)[None, :]).astype(dtype)


def body(integrals, occupied_energy, virtual_energy, partner_list, tile_lists):
    orbitals, slice_rows, aux_width = integrals.shape
    tile_width = TILE
    occ_count = lax.axis_size("occ")
    myself = lax.axis_index("occ")
    slice_id = lax.axis_index("virt")
    full_rows = virtual_energy.shape[0]
    a_count = slice_rows // tile_width
    b_count = full_rows // tile_width
    own_full = lax.all_gather(integrals, "virt", axis=1, tiled=True)
    spread = lax.all_to_all(
        split_pieces(own_full, occ_count), "occ", split_axis=1, concat_axis=1, tiled=True
    )
    outgoing = (
        jnp.take(spread, partner_list[0], axis=1),
        jnp.take(spread, partner_list[1], axis=1),
    )
    partner_one, partner_two = (
        lax.all_to_all(outgoing[0], "occ", split_axis=1, concat_axis=1, tiled=True),
        lax.all_to_all(outgoing[1], "occ", split_axis=1, concat_axis=1, tiled=True),
    )
    partners = (join_pieces(partner_one), join_pieces(partner_two))
    own_tiles = to_tiles(integrals, tile_width)
    own_energy = lax.dynamic_slice_in_dim(occupied_energy, myself * orbitals, orbitals, 0)
    energy_left = lax.dynamic_slice_in_dim(
        virtual_energy, slice_id * slice_rows, slice_rows, 0
    ).reshape(a_count, tile_width)
    energy_right = virtual_energy.reshape(b_count, tile_width)
    slot_count = tile_lists.shape[-1]
    group_size = math.gcd(slot_count, 16)
    highest = lax.Precision.HIGHEST
    totals = jnp.zeros((a_count, orbitals * tile_width, aux_width), jnp.float32)
    for pairing in range(2):
        partner_tiles = to_tiles(partners[pairing], tile_width)
        partner_energy = lax.dynamic_slice_in_dim(
            occupied_energy, partner_list[pairing, myself] * orbitals, orbitals, 0
        )
        listed = tile_lists[pairing, 0, 0]

        def group_step(
            number,
            running,
            listed=listed,
            partner_tiles=partner_tiles,
            partner_energy=partner_energy,
        ):
            entries = lax.dynamic_slice_in_dim(listed, number * group_size, group_size, 0)
            in_use = entries >= 0
            clamped = jnp.maximum(entries, 0)
            a_tile = clamped // b_count
            c_tile = clamped % b_count
            a_pick = one_hot(a_tile, a_count, jnp.bfloat16)
            c_pick = one_hot(c_tile, b_count, jnp.bfloat16)
            a_float = one_hot(a_tile, a_count, jnp.float32)
            c_float = one_hot(c_tile, b_count, jnp.float32)
            own_rows = jnp.einsum(
                "ga,axp->gxp", a_pick, own_tiles, preferred_element_type=jnp.float32
            ).astype(jnp.bfloat16)
            partner_rows = jnp.einsum(
                "gc,cyp->gyp", c_pick, partner_tiles, preferred_element_type=jnp.float32
            ).astype(jnp.bfloat16)
            scores = jnp.einsum(
                "gxp,gyp->gxy", own_rows, partner_rows, preferred_element_type=jnp.float32
            )
            left_rows = jnp.dot(a_float, energy_left, precision=highest)
            right_rows = jnp.dot(c_float, energy_right, precision=highest)
            gap_left = (left_rows[:, None, :] - own_energy[None, :, None]).reshape(
                group_size, orbitals * tile_width
            )
            gap_right = (right_rows[:, None, :] - partner_energy[None, :, None]).reshape(
                group_size, orbitals * tile_width
            )
            ratio = scores / (gap_left[:, :, None] + gap_right[:, None, :])
            amplitude = jnp.where(in_use[:, None, None], ratio, jnp.zeros_like(ratio)).astype(
                jnp.bfloat16
            )
            contrib = jnp.einsum(
                "gxy,gyp->gxp", amplitude, partner_rows, preferred_element_type=jnp.float32
            )
            return running + jnp.einsum("ga,gxp->axp", a_float, contrib, precision=highest)

        group_count = slot_count // group_size
        totals = lax.fori_loop(0, group_count, group_step, totals)
    shaped = totals.reshape(a_count, orbitals, tile_width, aux_width).transpose(1, 0, 2, 3)
    return shaped.reshape(orbitals, slice_rows, aux_width)


def solution(mesh):
    return jax.shard_map(
        body,
        mesh=mesh,
        in_specs=(P("occ", "virt", None), P(), P(), P(), P(None, "occ", "virt", None)),
        out_specs=P("occ", "virt", None),
        check_vma=False,
    )
```

profile of v0, /device:TPU:1, one launch (start us, length us, event | category | flops | bytes accessed | tf_op | source)
XLA Modules:
  0.0 559.1 jit_solution(15831569665805718759)
XLA Ops:
  7.3 41.2 %all-gather.2.cloned.1.call-done = bf16[1,1024,1536]{2,1,0:T(8,128)(2,1)} async-done(((bf16[1,256,1536]{2,1,0:T(8,128)(2,1)}), bf16[1,1024,1536]{2,1,0:T(8,128)(2,1)}) %all-gather.2.cloned.1.call-update) | async-done | bytes 3145744 | tf_op jit(solution)/shard_map/all_gather | solution.py:41
  48.5 10.3 %all-to-all-start = ((bf16[1,64,16,1536]{3,2,0,1:T(8,128)(2,1)}), bf16[1,64,16,1536]{3,2,0,1:T(8,128)(2,1)S(1)}, u32[]{:S(2)}, u32[]{:S(2)}) async-start(bf16[1,64,16,1536]{3,2,0,1:T(8,128)(2,1)} %bitcast.95), calls=%async_computation | async-start | bytes 6291456 | tf_op jit(solution)/shard_map/all_to_all | solution.py:42
  58.8 71.3 %all-to-all-done = bf16[1,64,16,1536]{3,2,0,1:T(8,128)(2,1)S(1)} async-done(((bf16[1,64,16,1536]{3,2,0,1:T(8,128)(2,1)}), bf16[1,64,16,1536]{3,2,0,1:T(8,128)(2,1)S(1)}, u32[]{:S(2)}, u32[]{:S(2)}) %all-to-all-start) | async-done | bytes 3145760 | tf_op jit(solution)/shard_map/all_to_all | solution.py:42
  130.2 2.4 gather_fusion.1
  132.5 3.9 fusion.90
  136.4 8.5 %all-to-all-start.2 = ((bf16[1,64,16,1536]{3,2,0,1:T(8,128)(2,1)}), bf16[1,64,16,1536]{3,2,0,1:T(8,128)(2,1)}, u32[]{:S(2)}, u32[]{:S(2)}) async-start(bf16[1,64,16,1536]{3,2,0,1:T(8,128)(2,1)} %fusion.90), calls=%async_computation.2 | async-start | bytes 6291456 | tf_op jit(solution)/shard_map/all_to_all | solution.py:51
  145.0 2.4 gather_fusion
  147.4 3.9 fusion.91
  151.3 64.8 %all-to-all-done.2 = bf16[1,64,16,1536]{3,2,0,1:T(8,128)(2,1)} async-done(((bf16[1,64,16,1536]{3,2,0,1:T(8,128)(2,1)}), bf16[1,64,16,1536]{3,2,0,1:T(8,128)(2,1)}, u32[]{:S(2)}, u32[]{:S(2)}) %all-to-all-start.2) | async-done | bytes 3145760 | tf_op jit(solution)/shard_map/all_to_all | solution.py:51
  216.1 8.5 %all-to-all-start.1 = ((bf16[1,64,16,1536]{3,2,0,1:T(8,128)(2,1)}), bf16[1,64,16,1536]{3,2,0,1:T(8,128)(2,1)}, u32[]{:S(2)}, u32[]{:S(2)}) async-start(bf16[1,64,16,1536]{3,2,0,1:T(8,128)(2,1)} %fusion.91), calls=%async_computation.1 | async-start | bytes 6291456 | tf_op jit(solution)/shard_map/all_to_all | solution.py:50
  231.5 5.3 copy.36
  236.8 58.3 %all-to-all-done.1 = bf16[1,64,16,1536]{3,2,0,1:T(8,128)(2,1)} async-done(((bf16[1,64,16,1536]{3,2,0,1:T(8,128)(2,1)}), bf16[1,64,16,1536]{3,2,0,1:T(8,128)(2,1)}, u32[]{:S(2)}, u32[]{:S(2)}) %all-to-all-start.1) | async-done | bytes 3145760 | tf_op jit(solution)/shard_map/all_to_all | solution.py:50
  295.1 5.3 copy.33
  300.4 124.1 %while.32 = (s32[]{:T(128)}, f32[4,64,1536]{2,0,1:T(4,128)S(1)}, s32[56]{0:T(128)S(1)}, bf16[4,64,1536]{2,0,1:T(4,128)(2,1)}, bf16[16,64,1536]{2,0,1:T(8,128)(2,...) while((s32[]{:T(128)}, f32[4,64,1536]{2,0,1:T(4,128)S(1)}, ...), condition=%wide.region_1.3_spmd.clone, body=%wide.region_0.0_spmd.clone.sunk | while | flops 273147328 | bytes 22820376 | solution.py:114
  302.1 2.6 convolution_convert_fusion.10
  306.5 5.3 fusion.151
  311.7 6.3 %fusion.152 = f32[4,64,1536]{2,0,1:T(4,128)S(1)} fusion(f32[8,64,1536]{2,1,0:T(8,128)} %fusion.151, f32[4,64,1536]{2,0,1:T(4,128)S(1)} %get-tuple-element.723, pred[]{:T(512)S(6)} %compare.9, s32[8]{0:T(128)S(1)} %get-tuple-element.708), kind=kOutput, calls=%fused_computation.39.clone.1 | convolution fusion | flops 38535200 | bytes 6291489 | tf_op jit(solution)/shard_map/while/body/eval_jaxpr/ga,gxp->axp/dot_general | solution.py:111
  319.8 2.6 convolution_convert_fusion.10
  322.4 1.8 convolution_convert_fusion.11
  324.2 5.3 fusion.151
  329.5 6.3 %fusion.152 = f32[4,64,1536]{2,0,1:T(4,128)S(1)} fusion(f32[8,64,1536]{2,1,0:T(8,128)} %fusion.151, f32[4,64,1536]{2,0,1:T(4,128)S(1)} %get-tuple-element.723, pred[]{:T(512)S(6)} %compare.9, s32[8]{0:T(128)S(1)} %get-tuple-element.708), kind=kOutput, calls=%fused_computation.39.clone.1 | convolution fusion | flops 38535200 | bytes 6291489 | tf_op jit(solution)/shard_map/while/body/eval_jaxpr/ga,gxp->axp/dot_general | solution.py:111
  337.5 2.6 convolution_convert_fusion.10
  340.1 1.8 convolution_convert_fusion.11
  341.9 5.3 fusion.151
  347.2 6.3 %fusion.152 = f32[4,64,1536]{2,0,1:T(4,128)S(1)} fusion(f32[8,64,1536]{2,1,0:T(8,128)} %fusion.151, f32[4,64,1536]{2,0,1:T(4,128)S(1)} %get-tuple-element.723, pred[]{:T(512)S(6)} %compare.9, s32[8]{0:T(128)S(1)} %get-tuple-element.708), kind=kOutput, calls=%fused_computation.39.clone.1 | convolution fusion | flops 38535200 | bytes 6291489 | tf_op jit(solution)/shard_map/while/body/eval_jaxpr/ga,gxp->axp/dot_general | solution.py:111
  355.3 2.6 convolution_convert_fusion.10
  357.9 1.8 convolution_convert_fusion.11
  359.6 5.3 fusion.151
  364.9 6.3 %fusion.152 = f32[4,64,1536]{2,0,1:T(4,128)S(1)} fusion(f32[8,64,1536]{2,1,0:T(8,128)} %fusion.151, f32[4,64,1536]{2,0,1:T(4,128)S(1)} %get-tuple-element.723, pred[]{:T(512)S(6)} %compare.9, s32[8]{0:T(128)S(1)} %get-tuple-element.708), kind=kOutput, calls=%fused_computation.39.clone.1 | convolution fusion | flops 38535200 | bytes 6291489 | tf_op jit(solution)/shard_map/while/body/eval_jaxpr/ga,gxp->axp/dot_general | solution.py:111
  373.0 2.6 convolution_convert_fusion.10
  375.6 1.8 convolution_convert_fusion.11
  377.4 5.3 fusion.151
  382.6 6.3 %fusion.152 = f32[4,64,1536]{2,0,1:T(4,128)S(1)} fusion(f32[8,64,1536]{2,1,0:T(8,128)} %fusion.151, f32[4,64,1536]{2,0,1:T(4,128)S(1)} %get-tuple-element.723, pred[]{:T(512)S(6)} %compare.9, s32[8]{0:T(128)S(1)} %get-tuple-element.708), kind=kOutput, calls=%fused_computation.39.clone.1 | convolution fusion | flops 38535200 | bytes 6291489 | tf_op jit(solution)/shard_map/while/body/eval_jaxpr/ga,gxp->axp/dot_general | solution.py:111
  390.7 2.6 convolution_convert_fusion.10
  393.3 1.8 convolution_convert_fusion.11
  395.1 5.3 fusion.151
  400.4 6.3 %fusion.152 = f32[4,64,1536]{2,0,1:T(4,128)S(1)} fusion(f32[8,64,1536]{2,1,0:T(8,128)} %fusion.151, f32[4,64,1536]{2,0,1:T(4,128)S(1)} %get-tuple-element.723, pred[]{:T(512)S(6)} %compare.9, s32[8]{0:T(128)S(1)} %get-tuple-element.708), kind=kOutput, calls=%fused_computation.39.clone.1 | convolution fusion | flops 38535200 | bytes 6291489 | tf_op jit(solution)/shard_map/while/body/eval_jaxpr/ga,gxp->axp/dot_general | solution.py:111
  408.4 2.6 convolution_convert_fusion.10
  411.0 1.8 convolution_convert_fusion.11
  412.8 5.3 fusion.151
  418.1 6.3 %fusion.152 = f32[4,64,1536]{2,0,1:T(4,128)S(1)} fusion(f32[8,64,1536]{2,1,0:T(8,128)} %fusion.151, f32[4,64,1536]{2,0,1:T(4,128)S(1)} %get-tuple-element.723, pred[]{:T(512)S(6)} %compare.9, s32[8]{0:T(128)S(1)} %get-tuple-element.708), kind=kOutput, calls=%fused_computation.39.clone.1 | convolution fusion | flops 38535200 | bytes 6291489 | tf_op jit(solution)/shard_map/while/body/eval_jaxpr/ga,gxp->axp/dot_general | solution.py:111
  424.4 126.2 %while.31 = (s32[]{:T(128)}, f32[4,64,1536]{2,0,1:T(4,128)S(1)}, s32[56]{0:T(128)S(1)}, bf16[4,64,1536]{2,0,1:T(4,128)(2,1)}, bf16[16,64,1536]{2,0,1:T(8,128)(2,...) while((s32[]{:T(128)}, f32[4,64,1536]{2,0,1:T(4,128)S(1)}, ...), condition=%wide.region_3.5_spmd, body=%wide.region_2.4_spmd.sunk | while | flops 272754112 | bytes 22820360 | solution.py:114
  426.4 2.6 convolution_convert_fusion.8
  430.8 5.2 fusion.138
  436.0 6.6 %fusion.139 = f32[4,64,1536]{2,0,1:T(4,128)S(1)} fusion(f32[4,64,1536]{2,0,1:T(4,128)S(1)} %get-tuple-element.762, f32[8,64,1536]{2,1,0:T(8,128)} %fusion.138, s32[8]{0:T(128)S(1)} %get-tuple-element.697), kind=kOutput, calls=%fused_computation.6.clone.1 | convolution fusion | flops 38141984 | bytes 6291488 | tf_op jit(solution)/shard_map/while/body/eval_jaxpr/ga,gxp->axp/dot_general | solution.py:111
  444.4 2.6 convolution_convert_fusion.8
  447.0 1.8 convolution_convert_fusion.9
  448.8 5.2 fusion.138
  454.0 6.6 %fusion.139 = f32[4,64,1536]{2,0,1:T(4,128)S(1)} fusion(f32[4,64,1536]{2,0,1:T(4,128)S(1)} %get-tuple-element.762, f32[8,64,1536]{2,1,0:T(8,128)} %fusion.138, s32[8]{0:T(128)S(1)} %get-tuple-element.697), kind=kOutput, calls=%fused_computation.6.clone.1 | convolution fusion | flops 38141984 | bytes 6291488 | tf_op jit(solution)/shard_map/while/body/eval_jaxpr/ga,gxp->axp/dot_general | solution.py:111
  462.4 2.6 convolution_convert_fusion.8
  466.8 5.2 fusion.138
  472.0 6.6 %fusion.139 = f32[4,64,1536]{2,0,1:T(4,128)S(1)} fusion(f32[4,64,1536]{2,0,1:T(4,128)S(1)} %get-tuple-element.762, f32[8,64,1536]{2,1,0:T(8,128)} %fusion.138, s32[8]{0:T(128)S(1)} %get-tuple-element.697), kind=kOutput, calls=%fused_computation.6.clone.1 | convolution fusion | flops 38141984 | bytes 6291488 | tf_op jit(solution)/shard_map/while/body/eval_jaxpr/ga,gxp->axp/dot_general | solution.py:111
  480.4 2.6 convolution_convert_fusion.8
  484.8 5.2 fusion.138
  490.0 6.6 %fusion.139 = f32[4,64,1536]{2,0,1:T(4,128)S(1)} fusion(f32[4,64,1536]{2,0,1:T(4,128)S(1)} %get-tuple-element.762, f32[8,64,1536]{2,1,0:T(8,128)} %fusion.138, s32[8]{0:T(128)S(1)} %get-tuple-element.697), kind=kOutput, calls=%fused_computation.6.clone.1 | convolution fusion | flops 38141984 | bytes 6291488 | tf_op jit(solution)/shard_map/while/body/eval_jaxpr/ga,gxp->axp/dot_general | solution.py:111
  498.4 2.6 convolution_convert_fusion.8
  502.8 5.2 fusion.138
  508.0 6.6 %fusion.139 = f32[4,64,1536]{2,0,1:T(4,128)S(1)} fusion(f32[4,64,1536]{2,0,1:T(4,128)S(1)} %get-tuple-element.762, f32[8,64,1536]{2,1,0:T(8,128)} %fusion.138, s32[8]{0:T(128)S(1)} %get-tuple-element.697), kind=kOutput, calls=%fused_computation.6.clone.1 | convolution fusion | flops 38141984 | bytes 6291488 | tf_op jit(solution)/shard_map/while/body/eval_jaxpr/ga,gxp->axp/dot_general | solution.py:111
  516.4 2.6 convolution_convert_fusion.8
  520.8 5.2 fusion.138
  526.0 6.6 %fusion.139 = f32[4,64,1536]{2,0,1:T(4,128)S(1)} fusion(f32[4,64,1536]{2,0,1:T(4,128)S(1)} %get-tuple-element.762, f32[8,64,1536]{2,1,0:T(8,128)} %fusion.138, s32[8]{0:T(128)S(1)} %get-tuple-element.697), kind=kOutput, calls=%fused_computation.6.clone.1 | convolution fusion | flops 38141984 | bytes 6291488 | tf_op jit(solution)/shard_map/while/body/eval_jaxpr/ga,gxp->axp/dot_general | solution.py:111
  534.4 2.6 convolution_convert_fusion.8
  538.8 5.2 fusion.138
  544.0 6.6 %fusion.139 = f32[4,64,1536]{2,0,1:T(4,128)S(1)} fusion(f32[4,64,1536]{2,0,1:T(4,128)S(1)} %get-tuple-element.762, f32[8,64,1536]{2,1,0:T(8,128)} %fusion.138, s32[8]{0:T(128)S(1)} %get-tuple-element.697), kind=kOutput, calls=%fused_computation.6.clone.1 | convolution fusion | flops 38141984 | bytes 6291488 | tf_op jit(solution)/shard_map/while/body/eval_jaxpr/ga,gxp->axp/dot_general | solution.py:111
  (115 shorter events, 42.1 us)
Async XLA Ops:
  6.5 41.9 %all-gather.2.cloned.1.call-start = ((), (), s32[]{:S(2)}) async-start(), calls=%async_computation.3 | async-start | bytes 3932160 | tf_op jit(solution)/shard_map/all_gather | solution.py:41
  48.5 10.3 %copy-start.5 = (s32[2,64]{1,0:T(2,128)S(1)}, s32[2,64]{1,0:T(2,128)}, u32[]{:S(2)}) copy-start(s32[2,64]{1,0:T(2,128)} %param.14) | copy-start | bytes 1540
  48.5 81.7 %all-to-all-start = ((bf16[1,64,16,1536]{3,2,0,1:T(8,128)(2,1)}), bf16[1,64,16,1536]{3,2,0,1:T(8,128)(2,1)S(1)}, u32[]{:S(2)}, u32[]{:S(2)}) async-start(bf16[1,64,16,1536]{3,2,0,1:T(8,128)(2,1)} %bitcast.95), calls=%async_computation | async-start | bytes 6291456 | tf_op jit(solution)/shard_map/all_to_all | solution.py:42
  136.4 79.7 %all-to-all-start.2 = ((bf16[1,64,16,1536]{3,2,0,1:T(8,128)(2,1)}), bf16[1,64,16,1536]{3,2,0,1:T(8,128)(2,1)}, u32[]{:S(2)}, u32[]{:S(2)}) async-start(bf16[1,64,16,1536]{3,2,0,1:T(8,128)(2,1)} %fusion.90), calls=%async_computation.2 | async-start | bytes 6291456 | tf_op jit(solution)/shard_map/all_to_all | solution.py:51
  151.3 76.5 %copy-start.3 = (f32[1024]{0:T(1024)S(1)}, f32[1024]{0:T(1024)}, u32[]{:S(2)}) copy-start(f32[1024]{0:T(1024)} %param.13) | copy-start | bytes 12292
  151.3 76.8 %copy-start.2 = (bf16[1,256,1536]{2,1,0:T(8,128)(2,1)S(1)}, bf16[1,256,1536]{2,1,0:T(8,128)(2,1)}, u32[]{:S(2)}) copy-start(bf16[1,256,1536]{2,1,0:T(8,128)(2,1)} %param.11) | copy-start | bytes 2359300
  216.1 79.0 %all-to-all-start.1 = ((bf16[1,64,16,1536]{3,2,0,1:T(8,128)(2,1)}), bf16[1,64,16,1536]{3,2,0,1:T(8,128)(2,1)}, u32[]{:S(2)}, u32[]{:S(2)}) async-start(bf16[1,64,16,1536]{3,2,0,1:T(8,128)(2,1)} %fusion.91), calls=%async_computation.1 | async-start | bytes 6291456 | tf_op jit(solution)/shard_map/all_to_all | solution.py:50
  224.6 6.2 %copy-start.4 = (f32[64]{0:T(128)S(1)}, f32[64]{0:T(128)}, u32[]{:S(2)}) copy-start(f32[64]{0:T(128)} %param.12) | copy-start | bytes 772
  224.6 6.9 %copy-start.6 = (s32[2,1,1,56]{3,2,1,0:T(1,128)S(1)}, s32[2,1,1,56]{3,2,1,0:T(1,128)}, u32[]{:S(2)}) copy-start(s32[2,1,1,56]{3,2,1,0:T(1,128)} %param.15) | copy-start | bytes 1348
  302.1 2.6 copy-start
  319.8 2.6 copy-start
  337.5 2.6 copy-start
  355.3 2.6 copy-start
  373.0 2.6 copy-start
  390.7 2.6 copy-start
  408.4 2.6 copy-start
  426.4 2.6 copy-start.1
  444.4 2.6 copy-start.1
  462.4 2.6 copy-start.1
  480.4 2.6 copy-start.1
  498.4 2.6 copy-start.1
  516.4 2.6 copy-start.1
  534.4 2.6 copy-start.1
Sparse Core Ops, SparseCore 0:
  9.1 39.2 all-gather.1
where the time goes:
time: 562 us; the launch traced here: 559 us
  matrix products  247 us (44%)
  waiting for transfers between devices  236 us (42%)
  starting transfers between devices  27.4 us (5%)
  local copies, waits for them, and re-layouts  20.1 us (4%)
  between operations  17.3 us (3%)
  other arithmetic  10 us (2%)
    dot_general x14, matrix products, group_step(): jnp.einsum('ga,gxp->axp', a_float, contrib, precision=highest)  90.7 us
    dot_general x14, matrix products, group_step(): jnp.einsum('gxy,gyp->gxp', amplitude, partner_rows, preferred_element_typ...  73.5 us
    all_to_all x1, waiting for transfers between devices, body(): lax.all_to_all(split_pieces(own_full, occ_count), 'occ', split_axis=1, co...  71.3 us
    all_to_all x1, waiting for transfers between devices, body(): lax.all_to_all(outgoing[1], 'occ', split_axis=1, concat_axis=1, tiled=True)  64.8 us
    all_to_all x1, waiting for transfers between devices, body(): lax.all_to_all(outgoing[0], 'occ', split_axis=1, concat_axis=1, tiled=True)  58.3 us
    all_gather x1, waiting for transfers between devices, body(): own_full = lax.all_gather(integrals, 'virt', axis=1, tiled=True)  41.2 us
    dot_general x14, matrix products, group_step(): jnp.einsum('gc,cyp->gyp', c_pick, partner_tiles, preferred_element_type=j...  36.3 us
    dot_general x14, matrix products, group_step(): jnp.einsum('ga,axp->gxp', a_pick, own_tiles, preferred_element_type=jnp.f...  24.9 us
  transfers between devices with their start and end apart: 4, of which 4 were waited for; matrix products, arithmetic and copies ran while one was open for 3% of the time, Pallas kernels for 0%

commit v1 on v0

v1 whole, which is shorter than its diff:
```python
import jax
import jax.numpy as jnp
from jax import lax
from jax.experimental import pallas as pl
from jax.experimental.pallas import tpu as pltpu
from jax.sharding import PartitionSpec as P

MESH = pl.DeviceIdType.MESH
TILE = 64
NY, NZ = 4, 8
BLOCKS = 64
PR, PC = 16, 384


def occ_of(l, y, z):
    return (y * NZ + z) * 2 + l


def z_step(idx):
    odd = lax.rem(idx, 2)
    return odd * lax.div(idx + 1, 2) + (1 - odd) * lax.rem(NZ - lax.div(idx, 2), NZ)


def kernel(
    plist, lists, gap_left, gap_right, own, out,
    recv1, send2, other, final, weights, hits,
    ss1, rs1, ss2, rsa, rso, ssx, rsx, ssc, rsc,
):
    occ = lax.axis_index("occ")
    virt = lax.axis_index("virt")
    l = lax.rem(occ, 2)
    z = lax.rem(lax.div(occ, 2), NZ)
    y = lax.div(occ, 2 * NZ)
    h = lax.div(virt, 2)
    c = lax.rem(virt, 2)
    hv = (1 - h) * 2 + c
    far = (occ, hv)
    near = (occ_of(1 - l, y, z), virt)
    cross = (occ_of(1 - l, y, z), hv)
    sibling = (occ, h * 2 + 1 - c)
    sib_virt = h * 2 + 1 - c
    sib_hv = (1 - h) * 2 + 1 - c

    def remote(src, dst, send, recv, device):
        return pltpu.make_async_remote_copy(
            src_ref=src, dst_ref=dst, send_sem=send, recv_sem=recv, device_id=device, device_id_type=MESH
        )

    barrier = pltpu.get_barrier_semaphore()

    def greet(q, carry):
        tl = lax.rem(l + lax.rem(q, 2), 2)
        ty = lax.rem(y + lax.rem(lax.div(q, 2), NY), NY)
        tz = lax.rem(z + lax.div(q, 2 * NY), NZ)
        pl.semaphore_signal(barrier, inc=1, device_id=(occ_of(tl, ty, tz), virt), device_id_type=MESH)
        return carry

    lax.fori_loop(1, BLOCKS, greet, 0)
    for device in (far, cross, sibling):
        pl.semaphore_signal(barrier, inc=1, device_id=device, device_id_type=MESH)
    pl.semaphore_wait(barrier, BLOCKS - 1 + 3)

    def piece(tl, ty, tz):
        row = pl.multiple_of((2 * tz + tl) * PR, PR)
        col = pl.multiple_of(ty * PC, 128)
        return own.at[pl.ds(row, PR), pl.ds(col, PC)]

    def spread(dz, q):
        tl = lax.rem(l + lax.rem(q, 2), 2)
        ty = lax.rem(y + lax.div(q, 2), NY)
        tz = lax.rem(z + dz, NZ)
        remote(piece(tl, ty, tz), recv1.at[occ], ss1, rs1, (occ_of(tl, ty, tz), virt)).start()

    def spread_group(n, carry):
        dz = z_step(NZ - 1 - n)

        def one(q, inner):
            spread(dz, q)
            return inner

        return lax.fori_loop(0, 2 * NY, one, carry)

    lax.fori_loop(0, NZ - 1, spread_group, 0)

    def spread_here(q, carry):
        spread(0, q)
        return carry

    lax.fori_loop(1, 2 * NY, spread_here, 0)
    pltpu.make_async_copy(piece(l, y, z), recv1.at[occ], rs1).start()

    out[...] = jnp.zeros_like(out)
    row_id = lax.broadcasted_iota(jnp.int32, (16, 256), 0)
    col_id = lax.broadcasted_iota(jnp.int32, (16, 256), 1)
    entry = lax.rem(row_id, 4) * 16 + lax.rem(lax.div(col_id, 32), 4) * 4 + lax.div(row_id, 4)
    first = col_id < 128
    slots = lists.shape[0] // 2

    def look(j, found):
        listed = jnp.where(first, lists[j], lists[slots + j])
        return jnp.where(entry == listed, jnp.float32(1), found)

    hits[...] = lax.fori_loop(0, slots, look, jnp.zeros((16, 256), jnp.float32))

    def weigh(zi, carry):
        right = gap_right[pl.ds(zi, 1), :]
        for a in range(4):
            rows = pl.ds(a * TILE, TILE)
            hit = hits[pl.ds(lax.div(zi, 2) * 4 + a, 1), :]
            weights[zi, rows, :] = hit / (gap_left[rows, :] + right)
        return carry

    lax.fori_loop(0, NZ, weigh, 0)

    pltpu.make_async_copy(recv1, recv1, rs1).wait()

    def pick(idx):
        tz = lax.rem(z + z_step(idx), NZ)

        def one(ty, carry):
            for tl in range(2):
                for k in range(2):
                    partner = plist[k * BLOCKS + occ_of(tl, ty, tz)]
                    send2[tz, ty, tl, k] = recv1[partner]
            return carry

        lax.fori_loop(0, NY, one, 0)

    def deliver(idx, first_y, sem):
        tz = lax.rem(z + z_step(idx), NZ)

        def one(dy, carry):
            ty = lax.rem(y + dy, NY)
            target = (occ_of(l, ty, tz), virt)
            remote(send2.at[tz, ty, l], final.at[:, virt, y, z, l], sem, rsa.at[idx], target).start()
            remote(send2.at[tz, ty, 1 - l], other.at[:, y, z], sem, rso.at[idx], target).start()
            return carry

        lax.fori_loop(first_y, NY, one, 0)

    pick(jnp.int32(0))
    pick(jnp.int32(1))
    pltpu.make_async_copy(send2.at[z, y, l], final.at[:, virt, y, z, l], rsa.at[0]).start()
    pltpu.make_async_copy(send2.at[z, y, 1 - l], other.at[:, y, z], rso.at[0]).start()
    deliver(jnp.int32(0), 1, ss2.at[0])

    def stage2(idx, carry):
        pick(idx + 1)
        deliver(idx, 0, ss2.at[1])
        return carry

    lax.fori_loop(1, NZ - 1, stage2, 0)
    deliver(jnp.int32(NZ - 1), 0, ss2.at[1])

    def await_(ref, sem):
        pltpu.make_async_copy(ref, ref, sem).wait()

    def step(t, carry):
        @pl.when(t < NZ)
        def _():
            zs = lax.rem(z - z_step(t) + NZ, NZ)
            mine = final.at[:, virt, :, zs, l]
            await_(mine, rsa.at[t])
            await_(other.at[:, :, zs], rso.at[t])
            remote(mine, mine, ssx, rsx.at[0, t], far).start()
            remote(other.at[:, :, zs], mine, ssx, rsx.at[1, t], near).start()
            remote(other.at[:, :, zs], mine, ssx, rsx.at[2, t], cross).start()
            remote(mine, mine, ssc, rsc.at[0, t], sibling).start()

        @pl.when((t >= 1) & (t < NZ + 1))
        def _():
            u = t - 1
            zs = lax.rem(z - z_step(u) + NZ, NZ)
            for n, place in enumerate((
                final.at[:, hv, :, zs, l], final.at[:, virt, :, zs, 1 - l], final.at[:, hv, :, zs, 1 - l],
            )):
                await_(place, rsx.at[n, u])
                remote(place, place, ssc, rsc.at[n + 1, u], sibling).start()

        @pl.when(t >= 2)
        def _():
            u = t - 2
            zs = lax.rem(z - z_step(u) + NZ, NZ)
            for n, place in enumerate((
                final.at[:, sib_virt, :, zs, l], final.at[:, sib_hv, :, zs, l],
                final.at[:, sib_virt, :, zs, 1 - l], final.at[:, sib_hv, :, zs, 1 - l],
            )):
                await_(place, rsc.at[n, u])
            rows = jnp.concatenate(
                [final[:, :, yi, zs].reshape(256, PC) for yi in range(NY)], axis=1
            )
            scores = lax.dot_general(
                own[...], rows, (((1,), (1,)), ((), ())), preferred_element_type=jnp.float32
            )
            amplitudes = (scores * weights[zs]).astype(jnp.bfloat16)
            out[...] += jnp.dot(amplitudes, rows, preferred_element_type=jnp.float32)

        return carry

    lax.fori_loop(0, NZ + 2, step, 0)

    await_(recv1.at[pl.ds(0, BLOCKS - 1)], ss1)
    await_(send2.at[0, pl.ds(0, NY - 1)], ss2.at[0])
    await_(send2.at[pl.ds(0, NZ - 1)], ss2.at[1])
    await_(final.at[0, pl.ds(0, 3)], ssx)
    await_(final.at[0], ssc)


def body(integrals, occupied_energy, virtual_energy, partner_list, tile_lists):
    _, rows, aux = integrals.shape
    myself = lax.axis_index("occ")
    slice_id = lax.axis_index("virt")
    slices = lax.axis_size("virt")
    bf16 = jnp.bfloat16
    left = lax.dynamic_slice_in_dim(virtual_energy, slice_id * rows, rows, 0) - occupied_energy[myself]
    right = virtual_energy.reshape(slices, NZ, 2 * PR).transpose(1, 0, 2).reshape(NZ, 1, slices * 2 * PR)
    partner_energy = occupied_energy[partner_list[:, myself]]
    right = (right - partner_energy[None, :, None]).reshape(NZ, 2 * slices * 2 * PR)
    dma = pltpu.SemaphoreType.DMA
    vmem = pl.BlockSpec(memory_space=pltpu.VMEM)
    smem = pl.BlockSpec(memory_space=pltpu.SMEM)
    gradient = pl.pallas_call(
        kernel,
        out_shape=jax.ShapeDtypeStruct((rows, aux), jnp.float32),
        in_specs=[smem, smem, vmem, vmem, vmem],
        out_specs=vmem,
        scratch_shapes=[
            pltpu.VMEM((BLOCKS, PR, PC), bf16),
            pltpu.VMEM((NZ, NY, 2, 2, PR, PC), bf16),
            pltpu.VMEM((2, NY, NZ, PR, PC), bf16),
            pltpu.VMEM((2, slices, NY, NZ, 2, PR, PC), bf16),
            pltpu.VMEM((NZ, rows, 2 * slices * 2 * PR), jnp.float32),
            pltpu.VMEM((16, 256), jnp.float32),
            dma, dma, dma((2,)), dma((NZ,)), dma((NZ,)), dma, dma((3, NZ)), dma, dma((4, NZ)),
        ],
        compiler_params=pltpu.CompilerParams(
            collective_id=0, has_side_effects=True, vmem_limit_bytes=48 * 1024 * 1024
        ),
        name="gradient",
    )(
        partner_list.reshape(-1), tile_lists.reshape(-1), left.reshape(rows, 1), right, integrals.reshape(rows, aux),
    )
    return gradient.reshape(1, rows, aux)


def solution(mesh):
    return jax.shard_map(
        body,
        mesh=mesh,
        in_specs=(P("occ", "virt", None), P(), P(), P(), P(None, "occ", "virt", None)),
        out_specs=P("occ", "virt", None),
        check_vma=False,
    )
```

time: 562 us -> 96.2 us (0.17)
  the two profiles are of different devices: /device:TPU:1 before, /device:TPU:81 now
where the time goes in v1:
time: 96.2 us; the launch traced here: 95.9 us
  Pallas kernels  85.1 us (88%)
  local copies, waits for them, and re-layouts  7.21 us (7%)
  other arithmetic  3.62 us (4%)
    pallas_call x1, Pallas kernels, body(): pl.pallas_call(kernel, out_shape=jax.ShapeDtypeStruct((rows, aux), jnp.fl...  85.1 us
    unnamed x4, local copies, waits for them, and re-layouts  2.79 us

profile of v1, /device:TPU:81, one launch (start us, length us, event | category | flops | bytes accessed | tf_op | source)
XLA Modules:
  0.0 95.9 jit_solution(6977082529187932351)
XLA Ops:
  0.0 1.2 %dynamic_slice.10 = f32[1]{0:T(128)} dynamic-slice(f32[64]{0:T(128)} %param.6, s32[]{:T(128)S(6)} %select_n.12), dynamic_slice_sizes={1} | dynamic-slice | bytes 12 | tf_op jit(solution)/shard_map/dynamic_slice | solution.py:215
  1.2 1.4 %dynamic-slice_subtract_fusion = f32[256]{0:T(256)S(1)} fusion(f32[1024]{0:T(1024)} %param.7, s32[]{:T(128)S(6)} %select_n.11, f32[]{:T(128)} %bitcast), kind=kLoop, calls=%fused_computation.5 | loop fusion | flops 256 | bytes 2056 | tf_op jit(solution)/shard_map/sub | solution.py:215
  2.6 0.9 fusion
  3.5 0.5 broadcast.24
  4.0 1.3 %reduce.5 = s32[2,56]{1,0:T(2,128)S(1)} reduce(s32[2,1,1,56]{3,2,1,0:T(1,128)} %param.9, s32[]{:T(128)} %broadcast.24), dimensions={1,2}, to_apply=%param.9.reduce_sub_computation.3 | reduce | bytes 900 | tf_op args[4]
  5.4 0.1 reshape.25.lists
  5.4 0.8 reshape.24.plist
  6.2 1.3 %gather_fusion = f32[2]{0:T(128)S(1)} fusion(f32[64]{0:T(128)} %param.6, s32[1024]{0:T(1024)S(1)} %pad_clamp_fusion), kind=kCustom, calls=%fused_computation | custom fusion | bytes 24 | tf_op jit(solution)/shard_map/gather | solution.py:217
  7.5 0.1 broadcast_bitcast_fusion
  7.6 0.8 reshape.27
  8.3 0.1 sub.30
  8.4 0.1 copy.8.gap_left
  8.6 0.0 copy-start
  8.6 1.1 %copy-done = bf16[1,256,1536]{2,1,0:T(8,128)(2,1)S(1)} copy-done((bf16[1,256,1536]{2,1,0:T(8,128)(2,1)S(1)}, bf16[1,256,1536]{2,1,0:T(8,128)(2,1)}, u32[]{:S(2)}) %copy-start) | copy-done | bytes 786456
  9.7 85.1 %gradient.1 = f32[256,1536]{1,0:T(8,128)S(1)} custom-call(s32[128]{0:T(128)S(1)} %reshape.24.plist, s32[112]{0:T(128)S(1)} %reshape.25.lists, f32[256,1]{1,0:T(8,128)S(1)} %copy.8.gap_left, f32[8,256]{1,0:T(8,128)S(1)} %bitcast_subtract_fusion.gap_right, bf16[256,1536]{1,0:T(8,128)(2,1)S(1)} %bitcast.10), custom_call_target="tpu_custom_call" | custom-call | tf_op jit(solution)/shard_map/gradient/pallas_call | solution.py:222
  94.8 1.1 %copy.10 = f32[1,256,1536]{2,1,0:T(8,128)} copy(f32[1,256,1536]{2,1,0:T(8,128)S(1)} %bitcast.9) | data formatting | bytes 3145728
  (3 shorter events, 0.0 us)
Async XLA Ops:
  8.6 1.1 %copy-start = (bf16[1,256,1536]{2,1,0:T(8,128)(2,1)S(1)}, bf16[1,256,1536]{2,1,0:T(8,128)(2,1)}, u32[]{:S(2)}) copy-start(bf16[1,256,1536]{2,1,0:T(8,128)(2,1)} %param.5) | copy-start | bytes 2359300

commit v2 on v1

v2 whole, which is shorter than its diff:
```python
import jax
import jax.numpy as jnp
from jax import lax
from jax.experimental import pallas as pl
from jax.experimental.pallas import tpu as pltpu
from jax.sharding import PartitionSpec as P

MESH = pl.DeviceIdType.MESH
TILE = 64
NY, NZ = 4, 8
BLOCKS = 64
HALVES = 2
PR, PC = 8, 384
STEPS = HALVES * NZ
SECOND = 2


def occ_of(l, y, z):
    return (y * NZ + z) * 2 + l


def z_step(idx):
    odd = lax.rem(idx, 2)
    return odd * lax.div(idx + 1, 2) + (1 - odd) * lax.rem(NZ - lax.div(idx, 2), NZ)


def kernel(
    plist_in, lists_in, occupied_in, virtual_in, integrals, out,
    plist, lists, occupied, virtual, own, recv_one, recv_two, send_one, send_two,
    other, final, weights, hits, gap_left, gap_right,
    load, ss1, rs1, ss2, rsa, rso, ssx, rsx, ssc, rsc,
):
    occ = lax.axis_index("occ")
    virt = lax.axis_index("virt")
    l = lax.rem(occ, 2)
    z = lax.rem(lax.div(occ, 2), NZ)
    y = lax.div(occ, 2 * NZ)
    h = lax.div(virt, 2)
    c = lax.rem(virt, 2)
    hv = (1 - h) * 2 + c
    far = (occ, hv)
    near = (occ_of(1 - l, y, z), virt)
    cross = (occ_of(1 - l, y, z), hv)
    sibling = (occ, h * 2 + 1 - c)
    sib_virt = h * 2 + 1 - c
    sib_hv = (1 - h) * 2 + 1 - c
    recv = (recv_one, recv_two)
    send = (send_one, send_two)

    def remote(src, dst, send_sem, recv_sem, device):
        return pltpu.make_async_remote_copy(
            src_ref=src, dst_ref=dst, send_sem=send_sem, recv_sem=recv_sem, device_id=device, device_id_type=MESH
        )

    fetches = [
        pltpu.make_async_copy(src, dst, load.at[n])
        for n, (src, dst) in enumerate((
            (integrals.at[0], own), (plist_in, plist), (lists_in, lists),
            (occupied_in, occupied), (virtual_in, virtual),
        ))
    ]
    for fetch in fetches:
        fetch.start()

    barrier = pltpu.get_barrier_semaphore()

    def greet(q, carry):
        tl = lax.rem(l + lax.rem(q, 2), 2)
        ty = lax.rem(y + lax.rem(lax.div(q, 2), NY), NY)
        tz = lax.rem(z + lax.div(q, 2 * NY), NZ)
        pl.semaphore_signal(barrier, inc=1, device_id=(occ_of(tl, ty, tz), virt), device_id_type=MESH)
        return carry

    lax.fori_loop(1, BLOCKS, greet, 0)
    for device in (far, cross, sibling):
        pl.semaphore_signal(barrier, inc=1, device_id=device, device_id_type=MESH)
    for fetch in fetches:
        fetch.wait()
    pl.semaphore_wait(barrier, BLOCKS - 1 + 3)

    def piece(half, tl, ty, tz):
        row = pl.multiple_of(half * 128 + (2 * tz + tl) * PR, PR)
        col = pl.multiple_of(ty * PC, 128)
        return own.at[pl.ds(row, PR), pl.ds(col, PC)]

    for half in range(HALVES):

        def spread(dz, q, half=half):
            tl = lax.rem(l + lax.rem(q, 2), 2)
            ty = lax.rem(y + lax.div(q, 2), NY)
            tz = lax.rem(z + dz, NZ)
            target = (occ_of(tl, ty, tz), virt)
            remote(piece(half, tl, ty, tz), recv[half].at[occ], ss1.at[half], rs1.at[half], target).start()

        def spread_group(n, carry, spread=spread):
            dz = z_step(NZ - 1 - n)

            def one(q, inner):
                spread(dz, q)
                return inner

            return lax.fori_loop(0, 2 * NY, one, carry)

        def spread_here(q, carry, spread=spread):
            spread(0, q)
            return carry

        lax.fori_loop(0, NZ - 1, spread_group, 0)
        lax.fori_loop(1, 2 * NY, spread_here, 0)
        pltpu.make_async_copy(piece(half, l, y, z), recv[half].at[occ], rs1.at[half]).start()

    out[...] = jnp.zeros_like(out)
    row_id = lax.broadcasted_iota(jnp.int32, (16, 128), 0)
    col_id = lax.broadcasted_iota(jnp.int32, (16, 128), 1)
    entry = lax.rem(row_id, 4) * 16 + lax.rem(lax.div(col_id, 16), 4) * 4 + lax.div(row_id, 4)
    first = col_id < 64
    slots = lists.shape[-1]

    def look(j, found):
        listed = jnp.where(first, lists[0, 0, 0, j], lists[1, 0, 0, j])
        return jnp.where(entry == listed, jnp.float32(1), found)

    hits[...] = lax.fori_loop(0, slots, look, jnp.zeros((16, 128), jnp.float32))
    for part in range(2):
        row = virtual[pl.ds(2 * virt + part, 1), :] - occupied[occ]
        gap_left[pl.ds(part * 128, 128), :] = jnp.transpose(jnp.broadcast_to(row, (128, 128)))
    lane = lax.broadcasted_iota(jnp.int32, (1, 128), 1)
    segment = lax.div(lane, 16)
    partner_energy = jnp.where(lane < 64, occupied[plist[0, occ]], occupied[plist[1, occ]])
    for half in range(HALVES):
        for zi in range(NZ):
            right = jnp.zeros((1, 128), jnp.float32)
            for g in range(8):
                row = virtual[2 * (g % 4) + half : 2 * (g % 4) + half + 1, :]
                shift = 16 * (g - zi) % 128
                right = jnp.where(segment == g, pltpu.roll(row, shift, 1) if shift else row, right)
            gap_right[half * NZ + zi : half * NZ + zi + 1, :] = right - partner_energy

    def weigh(n, carry):
        right = gap_right[pl.ds(n, 1), :]
        for a in range(4):
            rows = pl.ds(a * TILE, TILE)
            hit = hits[pl.ds(lax.div(n, 4) * 4 + a, 1), :]
            weights[n, rows, :] = hit / (gap_left[rows, :] + right)
        return carry

    lax.fori_loop(0, STEPS, weigh, 0)

    def stage2(half):
        def pick(idx):
            tz = lax.rem(z + z_step(idx), NZ)

            def one(ty, carry):
                for tl in range(2):
                    for k in range(2):
                        partner = plist[k, occ_of(tl, ty, tz)]
                        send[half][tz, ty, tl, k] = recv[half][partner]
                return carry

            lax.fori_loop(0, NY, one, 0)

        def deliver(idx, first_y, sem):
            tz = lax.rem(z + z_step(idx), NZ)

            def one(dy, carry):
                ty = lax.rem(y + dy, NY)
                target = (occ_of(l, ty, tz), virt)
                place = half * NZ + idx
                remote(
                    send[half].at[tz, ty, l], final.at[half, :, virt, y, z, l], sem, rsa.at[place], target
                ).start()
                remote(send[half].at[tz, ty, 1 - l], other.at[half, :, y, z], sem, rso.at[place], target).start()
                return carry

            lax.fori_loop(first_y, NY, one, 0)

        pltpu.make_async_copy(recv[half], recv[half], rs1.at[half]).wait()
        pick(jnp.int32(0))
        pick(jnp.int32(1))
        mine = rsa.at[half * NZ]
        pltpu.make_async_copy(send[half].at[z, y, l], final.at[half, :, virt, y, z, l], mine).start()
        theirs = rso.at[half * NZ]
        pltpu.make_async_copy(send[half].at[z, y, 1 - l], other.at[half, :, y, z], theirs).start()
        deliver(jnp.int32(0), 1, ss2.at[half, 0])

        def rest(idx, carry):
            pick(idx + 1)
            deliver(idx, 0, ss2.at[half, 1])
            return carry

        lax.fori_loop(1, NZ - 1, rest, 0)
        deliver(jnp.int32(NZ - 1), 0, ss2.at[half, 1])

    def await_(ref, sem):
        pltpu.make_async_copy(ref, ref, sem).wait()

    def source(u):
        return lax.rem(z - z_step(lax.rem(u, NZ)) + NZ, NZ)

    def rows_of(u):
        half = lax.div(u, NZ)
        zs = source(u)
        return jnp.concatenate(
            [final[half, :, :, yi, zs].reshape(128, PC) for yi in range(NY)], axis=1
        )

    def step(t, carry):
        @pl.when(t < STEPS)
        def _():
            half = lax.div(t, NZ)
            zs = source(t)
            mine = final.at[half, :, virt, :, zs, l]
            theirs = other.at[half, :, :, zs]
            await_(mine, rsa.at[t])
            await_(theirs, rso.at[t])
            remote(mine, mine, ssx, rsx.at[0, t], far).start()
            remote(theirs, mine, ssx, rsx.at[1, t], near).start()
            remote(theirs, mine, ssx, rsx.at[2, t], cross).start()
            remote(mine, mine, ssc, rsc.at[0, t], sibling).start()

        @pl.when((t >= 2) & (t < STEPS + 2))
        def _():
            u = t - 2
            half = lax.div(u, NZ)
            zs = source(u)
            for n, place in enumerate((
                final.at[half, :, hv, :, zs, l],
                final.at[half, :, virt, :, zs, 1 - l],
                final.at[half, :, hv, :, zs, 1 - l],
            )):
                await_(place, rsx.at[n, u])
                remote(place, place, ssc, rsc.at[n + 1, u], sibling).start()

        @pl.when((t >= 5) & (lax.rem(t, 2) == 1))
        def _():
            for u in (t - 5, t - 4):
                half = lax.div(u, NZ)
                zs = source(u)
                for n, place in enumerate((
                    final.at[half, :, sib_virt, :, zs, l],
                    final.at[half, :, sib_hv, :, zs, l],
                    final.at[half, :, sib_virt, :, zs, 1 - l],
                    final.at[half, :, sib_hv, :, zs, 1 - l],
                )):
                    await_(place, rsc.at[n, u])
            rows = jnp.concatenate([rows_of(t - 5), rows_of(t - 4)], axis=0)
            scores = lax.dot_general(
                own[...], rows, (((1,), (1,)), ((), ())), preferred_element_type=jnp.float32
            )
            scale = jnp.concatenate(
                [weights[lax.div(u, NZ) * NZ + source(u)] for u in (t - 5, t - 4)], axis=1
            )
            amplitudes = (scores * scale).astype(jnp.bfloat16)
            out[...] += jnp.dot(amplitudes, rows, preferred_element_type=jnp.float32)

        @pl.when(t == SECOND - 1)
        def _():
            stage2(1)

        return carry

    stage2(0)
    lax.fori_loop(0, STEPS + 4, step, 0)

    for half in range(HALVES):
        await_(recv[half].at[pl.ds(0, BLOCKS - 1)], ss1.at[half])
        await_(send[half].at[0, pl.ds(0, NY - 1)], ss2.at[half, 0])
        await_(send[half].at[pl.ds(0, NZ - 1)], ss2.at[half, 1])
    await_(final.at[0, :, pl.ds(0, 3)], ssx)
    await_(final.at[0], ssc)


def body(integrals, occupied_energy, virtual_energy, partner_list, tile_lists):
    _, rows, aux = integrals.shape
    slices = lax.axis_size("virt")
    bf16, f32 = jnp.bfloat16, jnp.float32
    dma = pltpu.SemaphoreType.DMA
    hbm = pl.BlockSpec(memory_space=pltpu.HBM)
    gradient = pl.pallas_call(
        kernel,
        out_shape=jax.ShapeDtypeStruct((rows, aux), f32),
        in_specs=[hbm] * 5,
        out_specs=pl.BlockSpec(memory_space=pltpu.VMEM),
        scratch_shapes=[
            pltpu.SMEM(partner_list.shape, jnp.int32),
            pltpu.SMEM(tile_lists.shape, jnp.int32),
            pltpu.SMEM(occupied_energy.shape, f32),
            pltpu.VMEM((8, 128), f32),
            pltpu.VMEM((rows, aux), bf16),
            pltpu.VMEM((BLOCKS, PR, PC), bf16),
            pltpu.VMEM((BLOCKS, PR, PC), bf16),
            pltpu.VMEM((NZ, NY, 2, 2, PR, PC), bf16),
            pltpu.VMEM((NZ, NY, 2, 2, PR, PC), bf16),
            pltpu.VMEM((HALVES, 2, NY, NZ, PR, PC), bf16),
            pltpu.VMEM((HALVES, 2, slices, NY, NZ, 2, PR, PC), bf16),
            pltpu.VMEM((STEPS, rows, 128), f32),
            pltpu.VMEM((16, 128), f32),
            pltpu.VMEM((rows, 128), f32),
            pltpu.VMEM((STEPS, 128), f32),
            dma((5,)), dma((HALVES,)), dma((HALVES,)), dma((HALVES, 2)), dma((STEPS,)), dma((STEPS,)),
            dma, dma((3, STEPS)), dma, dma((4, STEPS)),
        ],
        compiler_params=pltpu.CompilerParams(
            collective_id=0, has_side_effects=True, vmem_limit_bytes=48 * 1024 * 1024
        ),
        name="gradient",
    )(*[pltpu.with_memory_space_constraint(a, pltpu.HBM) for a in (partner_list, tile_lists, occupied_energy, virtual_energy.reshape(8, 128), integrals)])
    return gradient.reshape(1, rows, aux)


def solution(mesh):
    return jax.shard_map(
        body,
        mesh=mesh,
        in_specs=(P("occ", "virt", None), P(), P(), P(), P(None, "occ", "virt", None)),
        out_specs=P("occ", "virt", None),
        check_vma=False,
    )
```

time: 96.2 us -> 75.6 us (0.79)
  the two profiles are of different devices: /device:TPU:81 before, /device:TPU:1 now
where the time goes in v2:
time: 75.6 us
  Pallas kernels  74.4 us (98%)
  local copies, waits for them, and re-layouts  1.15 us (2%)
    pallas_call x1, Pallas kernels, body(): pl.pallas_call(kernel, out_shape=jax.ShapeDtypeStruct((rows, aux), f32),...  74.4 us

profile of v2, /device:TPU:1, one launch (start us, length us, event | category | flops | bytes accessed | tf_op | source)
XLA Modules:
  0.0 75.6 jit_solution(9822955151435499443)
XLA Ops:
  0.0 74.4 %gradient.1 = f32[256,1536]{1,0:T(8,128)S(1)} custom-call(s32[2,64]{1,0:T(2,128)} %plist_in.1, s32[2,1,1,56]{3,2,1,0:T(1,128)} %lists_in.1, f32[64]{0:T(128)} %occupied_in.1, f32[8,128]{1,0:T(8,128)} %bitcast.3, bf16[1,256,1536]{2,1,0:T(8,128)(2,1)} %integrals.1), custom_call_target="tpu_custom_call" | custom-call | tf_op jit(solution)/shard_map/gradient/pallas_call | solution.py:279
  74.4 1.1 %copy.7 = f32[1,256,1536]{2,1,0:T(8,128)} copy(f32[1,256,1536]{2,1,0:T(8,128)S(1)} %bitcast.2) | data formatting | bytes 3145728

commit v3 on v2

--- a/solution.py
+++ b/solution.py
@@ -28,7 +28,7 @@
     plist_in, lists_in, occupied_in, virtual_in, integrals, out,
     plist, lists, occupied, virtual, own, recv_one, recv_two, send_one, send_two,
     other, final, weights, hits, gap_left, gap_right,
-    load, ss1, rs1, ss2, rsa, rso, ssx, rsx, ssc, rsc,
+    load, ss1, rs1, ss2, rs2, ssx, rsx, ssc, rsc,
 ):
     occ = lax.axis_index("occ")
     virt = lax.axis_index("virt")
@@ -42,8 +42,6 @@
     near = (occ_of(1 - l, y, z), virt)
     cross = (occ_of(1 - l, y, z), hv)
     sibling = (occ, h * 2 + 1 - c)
-    sib_virt = h * 2 + 1 - c
-    sib_hv = (1 - h) * 2 + 1 - c
     recv = (recv_one, recv_two)
     send = (send_one, send_two)
 
@@ -64,14 +62,15 @@
 
     barrier = pltpu.get_barrier_semaphore()
 
-    def greet(q, carry):
+    def greet(n, carry):
+        tz = lax.rem(z + z_step(NZ - 1 - lax.div(n, 2 * NY)), NZ)
+        q = 2 * NY - 1 - lax.rem(n, 2 * NY)
         tl = lax.rem(l + lax.rem(q, 2), 2)
-        ty = lax.rem(y + lax.rem(lax.div(q, 2), NY), NY)
-        tz = lax.rem(z + lax.div(q, 2 * NY), NZ)
+        ty = lax.rem(y + lax.div(q, 2), NY)
         pl.semaphore_signal(barrier, inc=1, device_id=(occ_of(tl, ty, tz), virt), device_id_type=MESH)
         return carry
 
-    lax.fori_loop(1, BLOCKS, greet, 0)
+    lax.fori_loop(0, BLOCKS - 1, greet, 0)
     for device in (far, cross, sibling):
         pl.semaphore_signal(barrier, inc=1, device_id=device, device_id_type=MESH)
     for fetch in fetches:
@@ -167,9 +166,9 @@
                 target = (occ_of(l, ty, tz), virt)
                 place = half * NZ + idx
                 remote(
-                    send[half].at[tz, ty, l], final.at[half, :, virt, y, z, l], sem, rsa.at[place], target
+                    send[half].at[tz, ty, l], final.at[half, :, virt, y, z, l], sem, rs2.at[place], target
                 ).start()
-                remote(send[half].at[tz, ty, 1 - l], other.at[half, :, y, z], sem, rso.at[place], target).start()
+                remote(send[half].at[tz, ty, 1 - l], other.at[half, :, y, z], sem, rs2.at[place], target).start()
                 return carry
 
             lax.fori_loop(first_y, NY, one, 0)
@@ -177,10 +176,9 @@
         pltpu.make_async_copy(recv[half], recv[half], rs1.at[half]).wait()
         pick(jnp.int32(0))
         pick(jnp.int32(1))
-        mine = rsa.at[half * NZ]
-        pltpu.make_async_copy(send[half].at[z, y, l], final.at[half, :, virt, y, z, l], mine).start()
-        theirs = rso.at[half * NZ]
-        pltpu.make_async_copy(send[half].at[z, y, 1 - l], other.at[half, :, y, z], theirs).start()
+        here = rs2.at[half * NZ]
+        pltpu.make_async_copy(send[half].at[z, y, l], final.at[half, :, virt, y, z, l], here).start()
+        pltpu.make_async_copy(send[half].at[z, y, 1 - l], other.at[half, :, y, z], here).start()
         deliver(jnp.int32(0), 1, ss2.at[half, 0])
 
         def rest(idx, carry):
@@ -211,44 +209,34 @@
             zs = source(t)
             mine = final.at[half, :, virt, :, zs, l]
             theirs = other.at[half, :, :, zs]
-            await_(mine, rsa.at[t])
-            await_(theirs, rso.at[t])
-            remote(mine, mine, ssx, rsx.at[0, t], far).start()
-            remote(theirs, mine, ssx, rsx.at[1, t], near).start()
-            remote(theirs, mine, ssx, rsx.at[2, t], cross).start()
-            remote(mine, mine, ssc, rsc.at[0, t], sibling).start()
-
-        @pl.when((t >= 2) & (t < STEPS + 2))
+            await_(final.at[half, 0, 0, 0], rs2.at[t])
+            remote(mine, mine, ssx, rsx.at[t], far).start()
+            remote(theirs, mine, ssx, rsx.at[t], near).start()
+            remote(theirs, mine, ssx, rsx.at[t], cross).start()
+            remote(mine, mine, ssc, rsc.at[lax.div(t, 2)], sibling).start()
+
+        @pl.when((t >= 3) & (t < STEPS + 3))
         def _():
-            u = t - 2
+            u = t - 3
             half = lax.div(u, NZ)
             zs = source(u)
-            for n, place in enumerate((
+            await_(final.at[half, 0, 0, pl.ds(0, 3), pl.ds(0, 4)], rsx.at[u])
+            for place in (
                 final.at[half, :, hv, :, zs, l],
                 final.at[half, :, virt, :, zs, 1 - l],
                 final.at[half, :, hv, :, zs, 1 - l],
-            )):
-                await_(place, rsx.at[n, u])
-                remote(place, place, ssc, rsc.at[n + 1, u], sibling).start()
-
-        @pl.when((t >= 5) & (lax.rem(t, 2) == 1))
+            ):
+                remote(place, place, ssc, rsc.at[lax.div(u, 2)], sibling).start()
+
+        @pl.when((t >= 6) & (lax.rem(t, 2) == 0))
         def _():
-            for u in (t - 5, t - 4):
-                half = lax.div(u, NZ)
-                zs = source(u)
-                for n, place in enumerate((
-                    final.at[half, :, sib_virt, :, zs, l],
-                    final.at[half, :, sib_hv, :, zs, l],
-                    final.at[half, :, sib_virt, :, zs, 1 - l],
-                    final.at[half, :, sib_hv, :, zs, 1 - l],
-                )):
-                    await_(place, rsc.at[n, u])
-            rows = jnp.concatenate([rows_of(t - 5), rows_of(t - 4)], axis=0)
+            await_(final.at[0, 0, 0], rsc.at[lax.div(t - 6, 2)])
+            rows = jnp.concatenate([rows_of(t - 6), rows_of(t - 5)], axis=0)
             scores = lax.dot_general(
                 own[...], rows, (((1,), (1,)), ((), ())), preferred_element_type=jnp.float32
             )
             scale = jnp.concatenate(
-                [weights[lax.div(u, NZ) * NZ + source(u)] for u in (t - 5, t - 4)], axis=1
+                [weights[lax.div(u, NZ) * NZ + source(u)] for u in (t - 6, t - 5)], axis=1
             )
             amplitudes = (scores * scale).astype(jnp.bfloat16)
             out[...] += jnp.dot(amplitudes, rows, preferred_element_type=jnp.float32)
@@ -260,7 +248,7 @@
         return carry
 
     stage2(0)
-    lax.fori_loop(0, STEPS + 4, step, 0)
+    lax.fori_loop(0, STEPS + 5, step, 0)
 
     for half in range(HALVES):
         await_(recv[half].at[pl.ds(0, BLOCKS - 1)], ss1.at[half])
@@ -297,8 +285,8 @@
             pltpu.VMEM((16, 128), f32),
             pltpu.VMEM((rows, 128), f32),
             pltpu.VMEM((STEPS, 128), f32),
-            dma((5,)), dma((HALVES,)), dma((HALVES,)), dma((HALVES, 2)), dma((STEPS,)), dma((STEPS,)),
-            dma, dma((3, STEPS)), dma, dma((4, STEPS)),
+            dma((5,)), dma((HALVES,)), dma((HALVES,)), dma((HALVES, 2)), dma((STEPS,)),
+            dma, dma((STEPS,)), dma, dma((STEPS // 2,)),
         ],
         compiler_params=pltpu.CompilerParams(
             collective_id=0, has_side_effects=True, vmem_limit_bytes=48 * 1024 * 1024

time: 75.6 us -> 73.4 us (0.971)
  Pallas kernels: 74.4 us -> 72.2 us
    pallas_call x1, Pallas kernels: 74.4 us -> 72.2 us  [body(): pl.pallas_call(kernel, out_shape=jax.ShapeDtypeStruct((rows, aux), f32),...]
where the time goes in v3:
time: 73.4 us; the launch traced here: 73.3 us
  Pallas kernels  72.2 us (98%)
  local copies, waits for them, and re-layouts  1.15 us (2%)
    pallas_call x1, Pallas kernels, body(): pl.pallas_call(kernel, out_shape=jax.ShapeDtypeStruct((rows, aux), f32),...  72.2 us

profile of v3, /device:TPU:1, one launch (start us, length us, event | category | flops | bytes accessed | tf_op | source)
XLA Modules:
  0.0 73.3 jit_solution(7064363565706003883)
XLA Ops:
  0.0 72.2 %gradient.1 = f32[256,1536]{1,0:T(8,128)S(1)} custom-call(s32[2,64]{1,0:T(2,128)} %plist_in.1, s32[2,1,1,56]{3,2,1,0:T(1,128)} %lists_in.1, f32[64]{0:T(128)} %occupied_in.1, f32[8,128]{1,0:T(8,128)} %bitcast.3, bf16[1,256,1536]{2,1,0:T(8,128)(2,1)} %integrals.1), custom_call_target="tpu_custom_call" | custom-call | tf_op jit(solution)/shard_map/gradient/pallas_call | solution.py:267
  72.2 1.1 %copy.7 = f32[1,256,1536]{2,1,0:T(8,128)} copy(f32[1,256,1536]{2,1,0:T(8,128)S(1)} %bitcast.2) | data formatting | bytes 3145728

commit v4 on v3

--- a/solution.py
+++ b/solution.py
@@ -62,15 +62,23 @@
 
     barrier = pltpu.get_barrier_semaphore()
 
-    def greet(n, carry):
-        tz = lax.rem(z + z_step(NZ - 1 - lax.div(n, 2 * NY)), NZ)
-        q = 2 * NY - 1 - lax.rem(n, 2 * NY)
-        tl = lax.rem(l + lax.rem(q, 2), 2)
-        ty = lax.rem(y + lax.div(q, 2), NY)
-        pl.semaphore_signal(barrier, inc=1, device_id=(occ_of(tl, ty, tz), virt), device_id_type=MESH)
+    plane = [
+        (lax.rem(l + q % 2, 2), lax.rem(y + q // 2, NY)) for q in range(2 * NY)
+    ]
+    starts = [occ_of(tl, ty, 0) for tl, ty in plane]
+
+    def greet(occ_id):
+        pl.semaphore_signal(barrier, inc=1, device_id=(occ_id, virt), device_id_type=MESH)
+
+    def greet_plane(n, carry):
+        tz = lax.rem(z + z_step(NZ - 1 - n), NZ)
+        for q in reversed(range(2 * NY)):
+            greet(starts[q] + 2 * tz)
         return carry
 
-    lax.fori_loop(0, BLOCKS - 1, greet, 0)
+    lax.fori_loop(0, NZ - 1, greet_plane, 0)
+    for q in reversed(range(1, 2 * NY)):
+        greet(starts[q] + 2 * z)
     for device in (far, cross, sibling):
         pl.semaphore_signal(barrier, inc=1, device_id=device, device_id_type=MESH)
     for fetch in fetches:
@@ -84,28 +92,20 @@
 
     for half in range(HALVES):
 
-        def spread(dz, q, half=half):
-            tl = lax.rem(l + lax.rem(q, 2), 2)
-            ty = lax.rem(y + lax.div(q, 2), NY)
-            tz = lax.rem(z + dz, NZ)
-            target = (occ_of(tl, ty, tz), virt)
+        def spread(q, tz, half=half):
+            tl, ty = plane[q]
+            target = (starts[q] + 2 * tz, virt)
             remote(piece(half, tl, ty, tz), recv[half].at[occ], ss1.at[half], rs1.at[half], target).start()
 
-        def spread_group(n, carry, spread=spread):
-            dz = z_step(NZ - 1 - n)
-
-            def one(q, inner):
-                spread(dz, q)
-                return inner
-
-            return lax.fori_loop(0, 2 * NY, one, carry)
-
-        def spread_here(q, carry, spread=spread):
-            spread(0, q)
+        def spread_plane(n, carry, spread=spread):
+            tz = lax.rem(z + z_step(NZ - 1 - n), NZ)
+            for q in range(2 * NY):
+                spread(q, tz)
             return carry
 
-        lax.fori_loop(0, NZ - 1, spread_group, 0)
-        lax.fori_loop(1, 2 * NY, spread_here, 0)
+        lax.fori_loop(0, NZ - 1, spread_plane, 0)
+        for q in range(1, 2 * NY):
+            spread(q, z)
         pltpu.make_async_copy(piece(half, l, y, z), recv[half].at[occ], rs1.at[half]).start()
 
     out[...] = jnp.zeros_like(out)

time: 73.4 us -> 72.8 us (level)
  no operation moved by 1% of the time
where the time goes in v4:
time: 72.8 us; the launch traced here: 72.7 us
  Pallas kernels  71.5 us (98%)
  local copies, waits for them, and re-layouts  1.15 us (2%)
    pallas_call x1, Pallas kernels, body(): pl.pallas_call(kernel, out_shape=jax.ShapeDtypeStruct((rows, aux), f32),...  71.5 us

profile of v4, /device:TPU:1, one launch (start us, length us, event | category | flops | bytes accessed | tf_op | source)
XLA Modules:
  0.0 72.7 jit_solution(12449052391089095)
XLA Ops:
  0.0 71.5 %gradient.1 = f32[256,1536]{1,0:T(8,128)S(1)} custom-call(s32[2,64]{1,0:T(2,128)} %plist_in.1, s32[2,1,1,56]{3,2,1,0:T(1,128)} %lists_in.1, f32[64]{0:T(128)} %occupied_in.1, f32[8,128]{1,0:T(8,128)} %bitcast.3, bf16[1,256,1536]{2,1,0:T(8,128)(2,1)} %integrals.1), custom_call_target="tpu_custom_call" | custom-call | tf_op jit(solution)/shard_map/gradient/pallas_call | solution.py:267
  71.6 1.1 %copy.7 = f32[1,256,1536]{2,1,0:T(8,128)} copy(f32[1,256,1536]{2,1,0:T(8,128)S(1)} %bitcast.2) | data formatting | bytes 3145728

commit v5 on v4

--- a/solution.py
+++ b/solution.py
@@ -149,29 +149,22 @@
         def pick(idx):
             tz = lax.rem(z + z_step(idx), NZ)
 
-            def one(ty, carry):
+            for ty in range(NY):
                 for tl in range(2):
                     for k in range(2):
-                        partner = plist[k, occ_of(tl, ty, tz)]
+                        partner = plist[k, occ_of(tl, ty, 0) + 2 * tz]
                         send[half][tz, ty, tl, k] = recv[half][partner]
-                return carry
-
-            lax.fori_loop(0, NY, one, 0)
 
         def deliver(idx, first_y, sem):
             tz = lax.rem(z + z_step(idx), NZ)
 
-            def one(dy, carry):
-                ty = lax.rem(y + dy, NY)
-                target = (occ_of(l, ty, tz), virt)
-                place = half * NZ + idx
-                remote(
-                    send[half].at[tz, ty, l], final.at[half, :, virt, y, z, l], sem, rs2.at[place], target
-                ).start()
-                remote(send[half].at[tz, ty, 1 - l], other.at[half, :, y, z], sem, rs2.at[place], target).start()
-                return carry
-
-            lax.fori_loop(first_y, NY, one, 0)
+            place = half * NZ + idx
+            for dy in range(first_y, NY):
+                ty = plane[2 * dy][1]
+                target = (starts[2 * dy] + 2 * tz, virt)
+                arrival = rs2.at[place]
+                remote(send[half].at[tz, ty, l], final.at[half, :, virt, y, z, l], sem, arrival, target).start()
+                remote(send[half].at[tz, ty, 1 - l], other.at[half, :, y, z], sem, arrival, target).start()
 
         pltpu.make_async_copy(recv[half], recv[half], rs1.at[half]).wait()
         pick(jnp.int32(0))

time: 72.8 us -> 72.8 us (level)
  no operation moved by 1% of the time
where the time goes in v5:
time: 72.8 us; the launch traced here: 72.7 us
  Pallas kernels  71.5 us (98%)
  local copies, waits for them, and re-layouts  1.15 us (2%)
    pallas_call x1, Pallas kernels, body(): pl.pallas_call(kernel, out_shape=jax.ShapeDtypeStruct((rows, aux), f32),...  71.5 us

profile of v5, /device:TPU:1, one launch (start us, length us, event | category | flops | bytes accessed | tf_op | source)
XLA Modules:
  0.0 72.7 jit_solution(7136183279159059789)
XLA Ops:
  0.0 71.5 %gradient.1 = f32[256,1536]{1,0:T(8,128)S(1)} custom-call(s32[2,64]{1,0:T(2,128)} %plist_in.1, s32[2,1,1,56]{3,2,1,0:T(1,128)} %lists_in.1, f32[64]{0:T(128)} %occupied_in.1, f32[8,128]{1,0:T(8,128)} %bitcast.3, bf16[1,256,1536]{2,1,0:T(8,128)(2,1)} %integrals.1), custom_call_target="tpu_custom_call" | custom-call | tf_op jit(solution)/shard_map/gradient/pallas_call | solution.py:260
  71.6 1.1 %copy.7 = f32[1,256,1536]{2,1,0:T(8,128)} copy(f32[1,256,1536]{2,1,0:T(8,128)S(1)} %bitcast.2) | data formatting | bytes 3145728
